TPU v7x, 256 devices: a whole 4x4x8 slice. The times are simulated.
256 devices in a mesh: rep: 4 (over y), fsdp: 64 (over x, z, core).
Axes of the slice: x: 4, y: 4, z: 8, core: 2. Of those that a mesh axis runs over, the one named last changes fastest.
Arguments:
- activations: bfloat16 [65536, 512], P(('rep', 'fsdp')), may hold values from -6 to 6
- output_grads: bfloat16 [65536, 8192], P(('rep', 'fsdp'))
- master: float32 [8192, 512], P('fsdp'), may hold values from -6 to 6
- first_moment: float32 [8192, 512], P('fsdp'), may hold values from -4 to 4
- second_moment: float32 [8192, 512], P('fsdp'), may hold values from 0.2 to 2
Outputs:
- new_master: float32 [8192, 512], P('fsdp')
- new_first: float32 [8192, 512], P('fsdp')
- new_second: float32 [8192, 512], P('fsdp')
- params: bfloat16 [8192, 512], replicated
All inputs are finite; a program needn't handle non-finite values.
Results may differ from a plain program's by a relative error of at most 0.0004.
Values may be sent and summed in bfloat16 or wider, within the bound.
No kernel may reach another device: no remote copies, remote signals or barrier semaphores. Data moves between devices by JAX's collectives and lax.ppermute only.
A program may use at most 128 MiB of HBM per device.

v0:
```python
import jax
import jax.numpy as jnp
from jax import lax
from jax.sharding import PartitionSpec as P

dot_epsilon = 1e-06
beta_one = 0.9
beta_two = 0.95
adam_epsilon = 1e-08
learn_rate = 0.02
decay_rate = 0.1
contract_first = (((0,), (0,)), ((), ()))


def swapped(shard, axis, apart):
    return lax.ppermute(shard, axis, [(i, i ^ 1 << apart) for i in range(lax.axis_size(axis))])


def reversed_bits(number_in, bit_count):
    result = 0
    for position in range(bit_count):
        result = result << 1 | number_in >> position & 1
    return result


def local(activations, output_grads, master, first_moment, second_moment):
    grad_shard = lax.psum_scatter(
        lax.dot_general(
            output_grads, activations, contract_first, preferred_element_type=jnp.float32
        ),
        "fsdp",
        scatter_dimension=0,
        tiled=True,
    )
    replica_count = lax.axis_size("rep")
    level_total = replica_count.bit_length() - 1
    replica = lax.axis_index("rep")
    current = grad_shard
    for level_index in range(level_total):
        side_bit = replica >> level_index & 1
        low_side = side_bit == 0
        half_rows = current.shape[0] // 2
        lower_half = current[:half_rows]
        upper_half = current[half_rows:]
        kept_rows = jnp.where(low_side, lower_half, upper_half)
        outgoing = jnp.where(low_side, upper_half, lower_half)
        incoming = swapped(outgoing, "rep", level_index)
        left_vec = jnp.where(low_side, kept_rows, incoming)
        right_vec = jnp.where(low_side, incoming, kept_rows)
        partial_dots = jnp.stack(
            [
                jnp.sum(left_vec * right_vec),
                jnp.sum(left_vec * left_vec),
                jnp.sum(right_vec * right_vec),
            ]
        )
        totals = lax.psum(partial_dots, "fsdp")
        for inner_bit in range(level_index + 1):
            totals = totals + swapped(totals, "rep", inner_bit)
        left_coef = 1.0 - totals[0] / (2.0 * (totals[1] + dot_epsilon))
        right_coef = 1.0 - totals[0] / (2.0 * (totals[2] + dot_epsilon))
        current = left_coef * left_vec + right_coef * right_vec
    piece_rows = current.shape[0]
    gathered = lax.all_gather(current, "rep", axis=0, tiled=True)
    ordered = [
        gathered[
            reversed_bits(place, level_total)
            * piece_rows : (reversed_bits(place, level_total) + 1)
            * piece_rows
        ]
        for place in range(replica_count)
    ]
    combined = jnp.concatenate(ordered, axis=0)
    correct_one = 1.0 - (beta_one**50) ** 2
    correct_two = 1.0 - (beta_two**50) ** 2
    new_first = beta_one * first_moment + (1.0 - beta_one) * combined
    new_second = beta_two * second_moment + (1.0 - beta_two) * combined * combined
    update = (
        new_first / correct_one / (jnp.sqrt(new_second / correct_two) + adam_epsilon)
        + decay_rate * master
    )
    new_master = master - learn_rate * update
    params = lax.all_gather(new_master.astype(jnp.bfloat16), "fsdp", axis=0, tiled=True)
    return (new_master, new_first, new_second, params)


def solution(mesh):
    in_specs = (
        P(("rep", "fsdp"), None),
        P(("rep", "fsdp"), None),
        P("fsdp", None),
        P("fsdp", None),
        P("fsdp", None),
    )
    out_specs = (P("fsdp", None), P("fsdp", None), P("fsdp", None), P())
    return jax.shard_map(local, mesh=mesh, in_specs=in_specs, out_specs=out_specs, check_vma=False)
```

profile of v0, /device:TPU:1, one launch (start us, length us, event | category | flops | bytes accessed | tf_op | source)
XLA Modules:
  0.0 601.0 jit_solution(10944400333961210456)
XLA Ops:
  7.2 0.0 copy-start
  7.2 0.0 reduce-scatter.2.cloned.1.call-start
  7.2 0.9 copy-done
  8.1 10.3 %fusion.6 = f32[8192,512]{1,0:T(8,128)} fusion(bf16[256,8192]{1,0:T(8,128)(2,1)} %param.6, bf16[256,512]{1,0:T(8,128)(2,1)S(1)} %copy-done), kind=kOutput, calls=%fused_computation.27 | convolution fusion | flops 2147483648 | bytes 21233664 | tf_op jit(solution)/shard_map/dot_general | solution.py:28
  18.4 0.0 copy-start.1
  18.4 0.0 copy-start.2
  18.4 0.0 copy-start.3
  18.4 0.0 reduce-scatter.2.cloned.1.call-update
  18.4 0.0 all-gather.2.cloned.1.call-start
  18.5 189.2 %reduce-scatter.2.cloned.1.call-done = f32[128,512]{1,0:T(8,128)} async-done(((f32[8192,512]{1,0:T(8,128)}), f32[128,512]{1,0:T(8,128)}) %reduce-scatter.2.cloned.1.call-update) | async-done | bytes 262160 | tf_op jit(solution)/shard_map/reduce_scatter | solution.py:27
  207.7 1.0 slice_select_fusion
  208.7 0.9 collective-permute-start
  209.6 3.0 collective-permute-done
  212.6 1.6 multiply_reduce_fusion.2
  214.2 2.0 pad_maximum_fusion.1
  216.2 129.1 %psum.14 = f32[3]{0:T(128)S(1)} all-reduce(f32[3]{0:T(128)S(1)} %pad_maximum_fusion.1), channel_id=1, replica_groups=mesh['rep'=4,'fsdp'=64] {'fsdp'}, use_global_device_ids=true, to_apply=%region_4.5 | all-reduce | flops 3 | bytes 24 | tf_op jit(solution)/shard_map/psum | solution.py:57
  345.3 1.3 collective-permute-start.1
  346.6 1.2 collective-permute-done.1
  347.8 0.6 fusion.5
  351.0 2.6 collective-permute-start.2
  353.7 2.1 collective-permute-done.2
  355.7 0.6 multiply_reduce_fusion.5
  356.4 2.0 pad_maximum_fusion.2
  358.4 126.3 %psum.15 = f32[3]{0:T(128)S(1)} all-reduce(f32[3]{0:T(128)S(1)} %pad_maximum_fusion.2), channel_id=1, replica_groups=mesh['rep'=4,'fsdp'=64] {'fsdp'}, use_global_device_ids=true, to_apply=%region_8.9 | all-reduce | flops 3 | bytes 24 | tf_op jit(solution)/shard_map/psum | solution.py:57
  484.7 1.3 collective-permute-start.3
  486.0 1.2 collective-permute-done.3
  487.2 2.5 collective-permute-start.4
  489.7 1.3 collective-permute-done.4
  491.1 0.6 fusion.4
  494.3 9.5 %all_gather.6 = f32[128,512]{1,0:T(8,128)S(1)} all-gather(f32[32,512]{1,0:T(8,128)S(1)} %multiply_add_fusion.2), channel_id=1, replica_groups=mesh['rep'=4,'fsdp'=64] {'rep'}, dimensions={0}, use_global_device_ids=true | all-gather | bytes 327680 | tf_op jit(solution)/shard_map/all_gather | solution.py:64
  503.8 0.0 copy-done.1
  503.8 0.0 copy-done.2
  503.9 0.0 copy-done.3
  503.9 1.1 fusion.1
  504.9 0.0 all-gather.2.cloned.1.call-update
  504.9 81.9 %all-gather.2.cloned.1.call-done = bf16[8192,512]{1,0:T(8,128)(2,1)} async-done(((bf16[128,512]{1,0:T(8,128)(2,1)}), bf16[8192,512]{1,0:T(8,128)(2,1)}) %all-gather.2.cloned.1.call-update) | async-done | bytes 8388624 | tf_op jit(solution)/shard_map/all_gather | solution.py:83
  586.9 7.3 %copy.10 = bf16[8192,512]{1,0:T(8,128)(2,1)} copy(bf16[8192,512]{1,0:T(8,128)(2,1)} %all-gather.2.cloned.1.call-done) | data formatting | bytes 16777216
  (7 shorter events, 0.1 us)
Async XLA Ops:
  7.2 1.0 copy-start
  7.2 200.5 %reduce-scatter.2.cloned.1.call-start = ((), (), s32[]{:S(2)}) async-start(), calls=%async_computation.1 | async-start | bytes 17039360 | tf_op jit(solution)/shard_map/reduce_scatter | solution.py:27
  18.4 485.4 %copy-start.1 = (f32[128,512]{1,0:T(8,128)S(1)}, f32[128,512]{1,0:T(8,128)}, u32[]{:S(2)}) copy-start(f32[128,512]{1,0:T(8,128)} %param.7) | copy-start | bytes 786436
  18.4 485.4 %copy-start.2 = (f32[128,512]{1,0:T(8,128)S(1)}, f32[128,512]{1,0:T(8,128)}, u32[]{:S(2)}) copy-start(f32[128,512]{1,0:T(8,128)} %param.8) | copy-start | bytes 786436
  18.4 485.5 %copy-start.3 = (f32[128,512]{1,0:T(8,128)S(1)}, f32[128,512]{1,0:T(8,128)}, u32[]{:S(2)}) copy-start(f32[128,512]{1,0:T(8,128)} %param.9) | copy-start | bytes 786436
  18.4 568.4 %all-gather.2.cloned.1.call-start = ((), (), s32[]{:S(2)}) async-start(), calls=%async_computation.2 | async-start | bytes 8519680 | tf_op jit(solution)/shard_map/all_gather | solution.py:83
  208.7 3.9 collective-permute-start
  345.3 2.5 collective-permute-start.1
  351.0 4.7 collective-permute-start.2
  484.7 2.5 collective-permute-start.3
  487.2 3.9 collective-permute-start.4
Sparse Core Ops, SparseCore 0:
  18.6 189.1 reduce-scatter.1
  505.1 81.7 all-gather.1
where the time goes:
time: 601 us
  waiting for transfers between devices  280 us (47%)
  blocking collectives  265 us (44%)
  between operations  19.3 us (3%)
  matrix products  10.3 us (2%)
  local copies, waits for them, and re-layouts  9.44 us (2%)
  starting transfers between devices  8.68 us (1%)
  other arithmetic  8.38 us (1%)
    psum x2, blocking collectives, local(): totals = lax.psum(partial_dots, 'fsdp')  255 us
    reduce_scatter x1, waiting for transfers between devices, local(): lax.psum_scatter(lax.dot_general(output_grads, activations, contract_firs...  189 us
    all_gather x1, waiting for transfers between devices, local(): lax.all_gather(new_master.astype(jnp.bfloat16), 'fsdp', axis=0, tiled=True)  81.9 us
  transfers between devices with their start and end apart: 7, of which 7 were waited for; matrix products, arithmetic and copies ran while one was open for 0% of the time, Pallas kernels for 0%

commit v1 on v0

--- a/solution.py
+++ b/solution.py
@@ -10,6 +10,13 @@
 learn_rate = 0.02
 decay_rate = 0.1
 contract_first = (((0,), (0,)), ((), ()))
+
+
+def direct_skins(x_in, axis_name="fsdp"):
+    plain = tuple((x_in for _ in range(lax.psum(1, axis_name=axis_name))))
+    t1 = jnp.stack(plain, axis=0)
+    near = lax.all_to_all(t1, axis_name=axis_name, split_axis=0, concat_axis=0)
+    return jnp.concatenate(near, axis=0)
 
 
 def swapped(shard, axis, apart):
@@ -80,7 +87,7 @@
         + decay_rate * master
     )
     new_master = master - learn_rate * update
-    params = lax.all_gather(new_master.astype(jnp.bfloat16), "fsdp", axis=0, tiled=True)
+    params = direct_skins(new_master.astype(jnp.bfloat16))
     return (new_master, new_first, new_second, params)
 
 

time: 601 us -> 717 us (1.19)
  blocking collectives: 265 us -> 461 us
  waiting for transfers between devices: 280 us -> 198 us
    all_to_all x0 -> x1, blocking collectives: none -> 196 us  [direct_skins(): near = lax.all_to_all(t1, axis_name=axis_name, split_axis=0, concat_axis=0)]
    all_gather x1 -> x0, waiting for transfers between devices: 81.9 us -> none  [local(): lax.all_gather(new_master.astype(jnp.bfloat16), 'fsdp', axis=0, tiled=True)]
  transfers between devices with their start and end apart: 7 -> 6, of which waited for: 7 -> 6; matrix products, arithmetic and copies ran while one was open for 0% -> 0% of each run, Pallas kernels for 0% -> 0%
where the time goes in v1:
time: 717 us; the launch traced here: 716 us
  blocking collectives  461 us (64%)
  waiting for transfers between devices  198 us (28%)
  between operations  19.3 us (3%)
  local copies, waits for them, and re-layouts  10.4 us (1%)
  matrix products  10.3 us (1%)
  starting transfers between devices  8.64 us (1%)
  other arithmetic  8.34 us (1%)
    psum x2, blocking collectives, local(): totals = lax.psum(partial_dots, 'fsdp')  255 us
    all_to_all x1, blocking collectives, direct_skins(): near = lax.all_to_all(t1, axis_name=axis_name, split_axis=0, concat_axis=0)  196 us
    reduce_scatter x1, waiting for transfers between devices, local(): lax.psum_scatter(lax.dot_general(output_grads, activations, contract_firs...  189 us
  transfers between devices with their start and end apart: 6, of which 6 were waited for; matrix products, arithmetic and copies ran while one was open for 0% of the time, Pallas kernels for 0%

profile of v1, /device:TPU:1, one launch (start us, length us, event | category | flops | bytes accessed | tf_op | source)
XLA Modules:
  0.0 716.2 jit_solution(7639712770253166810)
XLA Ops:
  7.2 0.0 copy-start
  7.2 0.0 reduce-scatter.2.cloned.1.call-start
  7.2 0.9 copy-done
  8.1 10.3 %fusion.6 = f32[8192,512]{1,0:T(8,128)} fusion(bf16[256,8192]{1,0:T(8,128)(2,1)} %param.6, bf16[256,512]{1,0:T(8,128)(2,1)S(1)} %copy-done), kind=kOutput, calls=%fused_computation.27 | convolution fusion | flops 2147483648 | bytes 21233664 | tf_op jit(solution)/shard_map/dot_general | solution.py:35
  18.4 0.0 copy-start.1
  18.4 0.0 copy-start.2
  18.4 0.0 copy-start.3
  18.4 0.0 reduce-scatter.2.cloned.1.call-update
  18.4 189.3 %reduce-scatter.2.cloned.1.call-done = f32[128,512]{1,0:T(8,128)} async-done(((f32[8192,512]{1,0:T(8,128)}), f32[128,512]{1,0:T(8,128)}) %reduce-scatter.2.cloned.1.call-update) | async-done | bytes 262160 | tf_op jit(solution)/shard_map/reduce_scatter | solution.py:34
  207.7 1.0 slice_select_fusion
  208.7 0.9 collective-permute-start
  209.6 3.0 collective-permute-done
  212.6 1.6 multiply_reduce_fusion.2
  214.2 2.0 pad_maximum_fusion.1
  216.2 129.1 %psum.14 = f32[3]{0:T(128)S(1)} all-reduce(f32[3]{0:T(128)S(1)} %pad_maximum_fusion.1), channel_id=1, replica_groups=mesh['rep'=4,'fsdp'=64] {'fsdp'}, use_global_device_ids=true, to_apply=%region_4.5 | all-reduce | flops 3 | bytes 24 | tf_op jit(solution)/shard_map/psum | solution.py:64
  345.3 1.3 collective-permute-start.1
  346.6 1.2 collective-permute-done.1
  347.8 0.6 fusion.5
  351.0 2.6 collective-permute-start.2
  353.7 2.1 collective-permute-done.2
  355.7 0.6 multiply_reduce_fusion.5
  356.4 2.0 pad_maximum_fusion.2
  358.4 126.3 %psum.15 = f32[3]{0:T(128)S(1)} all-reduce(f32[3]{0:T(128)S(1)} %pad_maximum_fusion.2), channel_id=1, replica_groups=mesh['rep'=4,'fsdp'=64] {'fsdp'}, use_global_device_ids=true, to_apply=%region_8.9 | all-reduce | flops 3 | bytes 24 | tf_op jit(solution)/shard_map/psum | solution.py:64
  484.7 1.3 collective-permute-start.3
  486.0 1.2 collective-permute-done.3
  487.2 2.5 collective-permute-start.4
  489.7 1.3 collective-permute-done.4
  491.1 0.6 fusion.4
  494.3 9.5 %all_gather.3 = f32[128,512]{1,0:T(8,128)S(1)} all-gather(f32[32,512]{1,0:T(8,128)S(1)} %multiply_add_fusion.2), channel_id=1, replica_groups=mesh['rep'=4,'fsdp'=64] {'rep'}, dimensions={0}, use_global_device_ids=true | all-gather | bytes 327680 | tf_op jit(solution)/shard_map/all_gather | solution.py:71
  503.8 0.0 copy-done.1
  503.8 0.0 copy-done.2
  503.9 0.0 copy-done.3
  503.9 1.0 fusion.1
  504.9 1.0 stack.26
  505.9 196.2 %all_to_all.5 = bf16[64,128,512]{2,1,0:T(8,128)(2,1)} all-to-all(bf16[64,128,512]{2,1,0:T(8,128)(2,1)S(1)} %stack.26), channel_id=1, replica_groups=mesh['rep'=4,'fsdp'=64] {'fsdp'}, dimensions={0} | all-to-all | bytes 16777216 | tf_op jit(solution)/shard_map/all_to_all | solution.py:18
  702.1 7.3 %copy.10 = bf16[8192,512]{1,0:T(8,128)(2,1)} copy(bf16[8192,512]{1,0:T(8,128)(2,1)} %bitcast.13) | data formatting | bytes 16777216
  (7 shorter events, 0.1 us)
Async XLA Ops:
  7.2 1.0 copy-start
  7.2 200.5 %reduce-scatter.2.cloned.1.call-start = ((), (), s32[]{:S(2)}) async-start(), calls=%async_computation.2 | async-start | bytes 17039360 | tf_op jit(solution)/shard_map/reduce_scatter | solution.py:34
  18.4 485.4 %copy-start.1 = (f32[128,512]{1,0:T(8,128)S(1)}, f32[128,512]{1,0:T(8,128)}, u32[]{:S(2)}) copy-start(f32[128,512]{1,0:T(8,128)} %param.7) | copy-start | bytes 786436
  18.4 485.4 %copy-start.2 = (f32[128,512]{1,0:T(8,128)S(1)}, f32[128,512]{1,0:T(8,128)}, u32[]{:S(2)}) copy-start(f32[128,512]{1,0:T(8,128)} %param.8) | copy-start | bytes 786436
  18.4 485.5 %copy-start.3 = (f32[128,512]{1,0:T(8,128)S(1)}, f32[128,512]{1,0:T(8,128)}, u32[]{:S(2)}) copy-start(f32[128,512]{1,0:T(8,128)} %param.9) | copy-start | bytes 786436
  208.7 3.9 collective-permute-start
  345.3 2.5 collective-permute-start.1
  351.0 4.7 collective-permute-start.2
  484.7 2.5 collective-permute-start.3
  487.2 3.9 collective-permute-start.4
Sparse Core Ops, SparseCore 0:
  18.6 189.1 reduce-scatter.1
